TPU v7x, 128 devices: a whole 4x4x4 slice. The times are simulated.
128 devices in a mesh: dp: 4 (over y), expert: 32 (over x, z, core).
Axes of the slice: x: 4, y: 4, z: 4, core: 2. Of those that a mesh axis runs over, the one named last changes fastest.
Arguments:
- hidden_in: bfloat16 [32768, 1024], P(('dp', 'expert')), may hold values from -6 to 6
- moe_gain: float32 [1024], replicated, may hold values from 0.1 to 1.9
- router_weight: bfloat16 [1024, 64], replicated, may hold values from -0.1875 to 0.1875
- expert_gate: bfloat16 [64, 1024, 1024], P('expert'), may hold values from -0.1875 to 0.1875
- expert_up: bfloat16 [64, 1024, 1024], P('expert'), may hold values from -0.1875 to 0.1875
- expert_down: bfloat16 [64, 1024, 1024], P('expert'), may hold values from -0.1875 to 0.1875
- final_gain: float32 [1024], replicated, may hold values from 0.1 to 1.9
- vocab_weight: bfloat16 [1024, 32768], P(None, 'expert'), may hold values from -24 to 24
- token_ids: int32 [32768], P(('dp', 'expert')), may hold values from 0 to 32767
- doc_ids: int32 [32768], P(('dp', 'expert')), may hold values from 0 to 511, as said below
- routes: int32 [32768, 2], P(('dp', 'expert')), may hold values from 0 to 63, all different within a row; in each aligned block of 256 rows (0 to 255, 256 to 511, ...) at most 16 rows name the same one
Outputs:
- token_loss: float32 [32768], P(('dp', 'expert'))
- doc_score: float32 [512], P(('dp', 'expert'))
Inputs may be any that keep to these rules, and one draw needn't show every extreme that they name: `routes`: among the rows of one device no expert is named more than 16 times; in every draw some expert is named exactly 16 times by the rows of some device. `doc_ids`: documents are numbered in the order of the stream; each document is one run of consecutive tokens, shorter than 512; every document number is used; the rows of each device hold the first tokens of exactly 4 documents.
All inputs are finite; a program needn't handle non-finite values.
Results may differ from a plain program's by a relative error of at most 0.0031.
Values may be sent and summed in bfloat16 or wider, within the bound.
A program may use at most 128 MiB of HBM per device.

v0:
```python
import jax
import jax.numpy as jnp
from jax import lax
from jax.sharding import Mesh
from jax.sharding import PartitionSpec as P

TOP = 2
DOC_DEV = 4
EXPERT = ("expert_0", "expert_1", "expert_2")
DP_EXPERT = ("dp", "expert_0", "expert_1", "expert_2")
EPSILON = 1e-06


def shifted(value, axis, steps):
    count = lax.axis_size(axis)
    first, last = (max(0, -steps), min(count, count - steps))
    return lax.ppermute(value, axis, [(source, source + steps) for source in range(first, last)])


def gathered_once(value, axis):
    leaves = jax.tree.leaves(value)
    sequence = sorted(range(len(leaves)), key=lambda k: -leaves[k].size)
    width = (1, *leaves[sequence[0]].shape)[-1]
    lines = [
        jnp.pad(leaves[k].reshape(-1), (0, -leaves[k].size % width)).reshape(-1, width)
        for k in sequence
    ]
    both, at, found = (lax.all_gather(jnp.concatenate(lines), axis), 0, {})
    for k, line in zip(sequence, lines):
        slab = both[:, at : at + len(line)].reshape(len(both), -1)
        found[k] = slab[:, : leaves[k].size].reshape(-1, *leaves[k].shape)
        at += len(line)
    numbers = iter(range(len(leaves)))
    return jax.tree.map(lambda _: found[next(numbers)], value)


def merged_by_axis(value, axes, combine):
    for axis in axes:
        pieces = gathered_once(value, axis)
        value = jax.tree.map(lambda part: part[0], pieces)
        for k in range(1, lax.axis_size(axis)):
            value = combine(value, jax.tree.map(lambda part: part[k], pieces))
    return value


def by_axis(value, axes):
    for axis in axes:
        value = lax.psum(value, axis)
    return value


def normalize(values, gain_vector):
    inv_scale = lax.rsqrt(jnp.mean(values * values, axis=-1, keepdims=True) + EPSILON)
    return values * inv_scale * gain_vector


def stats_block(hidden_rows, wanted, vocab_weight, voc_start):
    scores = jnp.dot(hidden_rows, vocab_weight, preferred_element_type=jnp.float32)
    highest = jnp.max(scores, axis=1)
    totals = jnp.sum(jnp.exp(scores - highest[:, None]), axis=1)
    columns = voc_start + lax.broadcasted_iota(jnp.int32, scores.shape, 1)
    picked = jnp.sum(jnp.where(columns == wanted[:, None], scores, 0.0), axis=1)
    return (highest, totals, picked)


def row_stats(hidden_rows, wanted, vocab_weight, voc_start):
    row_count = hidden_rows.shape[0]

    def one_block(packed):
        return stats_block(packed[0], packed[1], vocab_weight, voc_start)

    blocks = lax.map(
        one_block,
        (
            hidden_rows.reshape(row_count // 1024, 1024, hidden_rows.shape[1]),
            wanted.reshape(row_count // 1024, 1024),
        ),
    )
    return tuple((member.reshape(row_count) for member in blocks))


def join_rows(first, second):
    highest = jnp.maximum(first[0], second[0])
    totals = first[1] * jnp.exp(first[0] - highest) + second[1] * jnp.exp(second[0] - highest)
    return (highest, totals, first[2] + second[2])


def local(
    hidden_in,
    moe_gain,
    router_weight,
    expert_gate,
    expert_up,
    expert_down,
    final_gain,
    vocab_weight,
    token_ids,
    doc_ids,
    routes,
):
    tok_rows, width = hidden_in.shape
    owners = lax.axis_size(EXPERT)
    local_experts = expert_gate.shape[0]
    experts = owners * local_experts
    slot_count = max(2, 2 * TOP * tok_rows // experts)
    residual = hidden_in.astype(jnp.float32)
    normed = normalize(residual, moe_gain).astype(jnp.bfloat16)
    router_scores = jnp.dot(normed, router_weight, preferred_element_type=jnp.float32)
    chosen = routes[:, :, None] == lax.broadcasted_iota(jnp.int32, (tok_rows, TOP, experts), 2)
    picked_scores = jnp.sum(jnp.where(chosen, router_scores[:, None, :], 0.0), axis=2)
    first_gate = jax.nn.sigmoid(picked_scores[:, 0] - picked_scores[:, 1])
    second_gate = 1.0 - first_gate
    flat_routes = routes.reshape(tok_rows * TOP)
    one_hot = (
        flat_routes[:, None] == lax.broadcasted_iota(jnp.int32, (tok_rows * TOP, experts), 1)
    ).astype(jnp.int32)
    slot_index = jnp.sum(one_hot * jnp.cumsum(one_hot, axis=0), axis=1) - 1
    position = flat_routes * slot_count + slot_index
    slot_iota = lax.broadcasted_iota(jnp.int32, (tok_rows * TOP, experts * slot_count), 1)
    placement = (
        (position[:, None] == slot_iota)
        .astype(jnp.bfloat16)
        .reshape(tok_rows, TOP, experts * slot_count)
    )
    first_place = placement[:, 0, :]
    second_place = placement[:, 1, :]
    dispatch_map = first_place + second_place
    outgoing = lax.dot_general(
        dispatch_map, normed, (((0,), (0,)), ((), ())), preferred_element_type=jnp.float32
    )
    outgoing = outgoing.astype(jnp.bfloat16).reshape(owners, local_experts, slot_count, width)
    arrived = lax.all_to_all(outgoing, EXPERT, split_axis=0, concat_axis=0, tiled=True)
    gate_part = jnp.einsum(
        "sekd,edf->sekf", arrived, expert_gate, preferred_element_type=jnp.float32
    )
    up_part = jnp.einsum("sekd,edf->sekf", arrived, expert_up, preferred_element_type=jnp.float32)
    active = (jax.nn.silu(gate_part) * up_part).astype(jnp.bfloat16)
    expert_result = jnp.einsum(
        "sekf,efd->sekd", active, expert_down, preferred_element_type=jnp.float32
    ).astype(jnp.bfloat16)
    returned = lax.all_to_all(
        expert_result, EXPERT, split_axis=0, concat_axis=0, tiled=True
    ).reshape(experts * slot_count, width)
    first_rows = jnp.dot(first_place, returned, preferred_element_type=jnp.float32)
    second_rows = jnp.dot(second_place, returned, preferred_element_type=jnp.float32)
    mixed = residual + (first_gate[:, None] * first_rows + second_gate[:, None] * second_rows)
    final_rows = normalize(mixed, final_gain).astype(jnp.bfloat16)
    following = shifted((token_ids[:1], doc_ids[:1]), DP_EXPERT, -1)
    targets = jnp.concatenate([token_ids[1:], following[0]])
    counted = jnp.concatenate([doc_ids[1:], following[1]]) == doc_ids
    voc_start = lax.axis_index(EXPERT) * vocab_weight.shape[1]
    fresh = row_stats(
        lax.all_gather(final_rows, EXPERT, axis=0, tiled=True),
        lax.all_gather(targets, EXPERT, axis=0, tiled=True),
        vocab_weight,
        voc_start,
    )
    row_highest, row_totals, row_picked = tuple((update for update in fresh))
    own_start = lax.axis_index(EXPERT) * tok_rows
    merged = merged_by_axis((row_highest, row_totals, row_picked), EXPERT, join_rows)
    own_high = lax.dynamic_slice_in_dim(merged[0], own_start, tok_rows, 0)
    own_totals = lax.dynamic_slice_in_dim(merged[1], own_start, tok_rows, 0)
    target_score = lax.dynamic_slice_in_dim(merged[2], own_start, tok_rows, 0)
    log_norm = own_high + jnp.log(own_totals)
    token_loss = jnp.where(counted, log_norm - target_score, 0.0)
    devices = lax.axis_size("dp") * owners
    documents = DOC_DEV * devices
    doc_start = (lax.axis_index("dp") * owners + lax.axis_index(EXPERT)) * DOC_DEV
    member_map = (
        doc_ids[:, None] == lax.broadcasted_iota(jnp.int32, (tok_rows, documents), 1)
    ).astype(jnp.float32)
    partial_loss = jnp.dot(token_loss, member_map, precision=lax.Precision.HIGHEST)
    partial_length = jnp.sum(member_map, axis=0)
    whole_loss, whole_length = (
        by_axis(partial_loss, DP_EXPERT),
        by_axis(partial_length, DP_EXPERT),
    )
    loss_sum = jnp.sum(whole_loss)
    doc_loss = lax.dynamic_slice_in_dim(whole_loss, doc_start, DOC_DEV, 0)
    doc_length = lax.dynamic_slice_in_dim(whole_length, doc_start, DOC_DEV, 0)
    global_mean = loss_sum / (tok_rows * devices - documents)
    doc_score = doc_loss / doc_length - global_mean
    return (token_loss, doc_score)


def solution(mesh):
    split = Mesh(
        mesh.devices.reshape(mesh.shape["dp"], 4, 4, 2), ("dp", "expert_0", "expert_1", "expert_2")
    )
    in_specs = (
        P(DP_EXPERT, None),
        P(),
        P(),
        P(EXPERT, None, None),
        P(EXPERT, None, None),
        P(EXPERT, None, None),
        P(),
        P(None, EXPERT),
        P(DP_EXPERT),
        P(DP_EXPERT),
        P(DP_EXPERT, None),
    )
    out_specs = (P(DP_EXPERT), P(DP_EXPERT))
    return jax.shard_map(local, mesh=split, in_specs=in_specs, out_specs=out_specs, check_vma=False)
```

profile of v0, /device:TPU:1, one launch (start us, length us, event | category | flops | bytes accessed | tf_op | source)
XLA Modules:
  0.0 299.3 jit_solution(4102769667074141839)
XLA Ops:
  14.7 37.4 %all_to_all.10 = bf16[32,2,16,1024]{3,2,1,0:T(8,128)(2,1)S(1)} all-to-all(bf16[32,2,16,1024]{3,2,1,0:T(8,128)(2,1)S(1)} %bitcast.274), channel_id=1, replica_groups=mesh['dp'=4,'expert_0'=4,'expert_1'=4,'expert_2'=2] {'expert_0','expert_..., dimensions={0} | all-to-all | bytes 4194304 | tf_op jit(solution)/shard_map/all_to_all | solution.py:132
  52.0 4.3 %fusion.8 = f32[2,32,16,1024]{3,2,1,0:T(8,128)} fusion(bf16[2,1024,1024]{2,1,0:T(8,128)(2,1)S(1)} %copy-done.7, bf16[32,2,16,1024]{3,2,1,0:T(8,128)(2,1)S(1)} %all_to_all.10), kind=kOutput, calls=%fused_computation.12 | convolution fusion | flops 2147483648 | bytes 10485760 | tf_op jit(solution)/shard_map/sekd,edf->sekf/dot_general | solution.py:133
  56.4 10.7 %convert_bitcast_fusion = bf16[32,2,16,1024]{3,2,0,1:T(8,128)(2,1)} fusion(bf16[2,1024,1024]{2,1,0:T(8,128)(2,1)} %param.18, f32[2,32,16,1024]{3,2,1,0:T(8,128)} %fusion.8, bf16[2,1024,1024]{2,1,0:T(8,128)(2,1)} %param.17, bf16[32,2,16,1024]{3,2,1,0:T(8,128)(2,1)S(1)} %all_to_all.10), kind=kOutput, calls=%fused_computation.21 | convolution fusion | flops 4302307328 | bytes 16777216 | tf_op jit(solution)/shard_map/sekf,efd->sekd/dot_general | solution.py:138
  67.0 3.3 %copy.53 = bf16[32,2,16,1024]{3,2,1,0:T(8,128)(2,1)} copy(bf16[32,2,16,1024]{3,2,0,1:T(8,128)(2,1)} %convert_bitcast_fusion) | data formatting | bytes 4194304 | tf_op jit(solution)/shard_map/convert_element_type | solution.py:140
  70.4 3.9 %all-to-all-start.1 = ((bf16[32,2,16,1024]{3,2,1,0:T(8,128)(2,1)}), bf16[32,2,16,1024]{3,2,1,0:T(8,128)(2,1)S(1)}, u32[]{:S(2)}, u32[]{:S(2)}) async-start(bf16[32,2,16,1024]{3,2,1,0:T(8,128)(2,1)} %copy.53), calls=%async_computation.1 | async-start | bytes 4194304 | tf_op jit(solution)/shard_map/all_to_all | solution.py:141
  74.8 27.8 %all-to-all-done.1 = bf16[32,2,16,1024]{3,2,1,0:T(8,128)(2,1)S(1)} async-done(((bf16[32,2,16,1024]{3,2,1,0:T(8,128)(2,1)}), bf16[32,2,16,1024]{3,2,1,0:T(8,128)(2,1)S(1)}, u32[]{:S(2)}, u32[]{:S(2)}) %all-to-all-start.1) | async-done | bytes 2097184 | tf_op jit(solution)/shard_map/all_to_all | solution.py:141
  112.1 24.1 %all-gather.3 = s32[32,1,256]{2,1,0:T(1,128)S(1)} all-gather(s32[1,1,256]{2,1,0:T(1,128)S(1)} %bitcast.293), channel_id=1, replica_groups=mesh['dp'=4,'expert_0'=4,'expert_1'=4,'expert_2'=2] {'expert_0','expert_..., dimensions={0}, use_global_device_ids=true | all-gather | bytes 33792 | tf_op jit(solution)/shard_map/all_gather | solution.py:154
  136.4 39.9 %all-gather.9.cloned.1.call-done = bf16[8192,1024]{1,0:T(8,128)(2,1)} async-done(((bf16[256,1024]{1,0:T(8,128)(2,1)}), bf16[8192,1024]{1,0:T(8,128)(2,1)}) %all-gather.9.cloned.1.call-update) | async-done | bytes 16777232 | tf_op jit(solution)/shard_map/all_gather | solution.py:153
  176.2 52.1 %while.14 = (s32[]{:T(128)}, f32[8,1024]{1,0:T(8,128)S(1)}, f32[8,1024]{1,0:T(8,128)S(1)}, f32[8,1024]{1,0:T(8,128)S(1)}, bf16[8,1024,1024]{2,1,0:T(8,128)(2,1)}...) while((s32[]{:T(128)}, f32[8,1024]{1,0:T(8,128)S(1)}, ...), condition=%wide.region_10.11_spmd, body=%wide.region_6.10_spmd.sunk | while | flops 2153773056 | bytes 12644985 | solution.py:72
  176.2 4.7 %fusion.87 = (f32[1024]{0:T(1024)S(1)}, f32[1024,1024]{0,1:T(8,128)S(1)}) fusion(bf16[1024,1024]{1,0:T(8,128)(2,1)} %get-tuple-element.175, bf16[8,1024,1024]{2,1,0:T(8,128)(2,1)} %get-tuple-element.174, s32[]{:T(128)} %get-tuple-element.160), kind=kOutput, calls=%fused_computation.133.clone.1 | convolution fusion | flops 2148531200 | bytes 8393216 | tf_op jit(solution)/shard_map/while/body/eval_jaxpr/dot_general | solution.py:58
  182.8 4.7 %fusion.87 = (f32[1024]{0:T(1024)S(1)}, f32[1024,1024]{0,1:T(8,128)S(1)}) fusion(bf16[1024,1024]{1,0:T(8,128)(2,1)} %get-tuple-element.175, bf16[8,1024,1024]{2,1,0:T(8,128)(2,1)} %get-tuple-element.174, s32[]{:T(128)} %get-tuple-element.160), kind=kOutput, calls=%fused_computation.133.clone.1 | convolution fusion | flops 2148531200 | bytes 8393216 | tf_op jit(solution)/shard_map/while/body/eval_jaxpr/dot_general | solution.py:58
  189.3 4.7 %fusion.87 = (f32[1024]{0:T(1024)S(1)}, f32[1024,1024]{0,1:T(8,128)S(1)}) fusion(bf16[1024,1024]{1,0:T(8,128)(2,1)} %get-tuple-element.175, bf16[8,1024,1024]{2,1,0:T(8,128)(2,1)} %get-tuple-element.174, s32[]{:T(128)} %get-tuple-element.160), kind=kOutput, calls=%fused_computation.133.clone.1 | convolution fusion | flops 2148531200 | bytes 8393216 | tf_op jit(solution)/shard_map/while/body/eval_jaxpr/dot_general | solution.py:58
  195.8 4.7 %fusion.87 = (f32[1024]{0:T(1024)S(1)}, f32[1024,1024]{0,1:T(8,128)S(1)}) fusion(bf16[1024,1024]{1,0:T(8,128)(2,1)} %get-tuple-element.175, bf16[8,1024,1024]{2,1,0:T(8,128)(2,1)} %get-tuple-element.174, s32[]{:T(128)} %get-tuple-element.160), kind=kOutput, calls=%fused_computation.133.clone.1 | convolution fusion | flops 2148531200 | bytes 8393216 | tf_op jit(solution)/shard_map/while/body/eval_jaxpr/dot_general | solution.py:58
  202.3 4.7 %fusion.87 = (f32[1024]{0:T(1024)S(1)}, f32[1024,1024]{0,1:T(8,128)S(1)}) fusion(bf16[1024,1024]{1,0:T(8,128)(2,1)} %get-tuple-element.175, bf16[8,1024,1024]{2,1,0:T(8,128)(2,1)} %get-tuple-element.174, s32[]{:T(128)} %get-tuple-element.160), kind=kOutput, calls=%fused_computation.133.clone.1 | convolution fusion | flops 2148531200 | bytes 8393216 | tf_op jit(solution)/shard_map/while/body/eval_jaxpr/dot_general | solution.py:58
  208.8 4.7 %fusion.87 = (f32[1024]{0:T(1024)S(1)}, f32[1024,1024]{0,1:T(8,128)S(1)}) fusion(bf16[1024,1024]{1,0:T(8,128)(2,1)} %get-tuple-element.175, bf16[8,1024,1024]{2,1,0:T(8,128)(2,1)} %get-tuple-element.174, s32[]{:T(128)} %get-tuple-element.160), kind=kOutput, calls=%fused_computation.133.clone.1 | convolution fusion | flops 2148531200 | bytes 8393216 | tf_op jit(solution)/shard_map/while/body/eval_jaxpr/dot_general | solution.py:58
  215.3 4.7 %fusion.87 = (f32[1024]{0:T(1024)S(1)}, f32[1024,1024]{0,1:T(8,128)S(1)}) fusion(bf16[1024,1024]{1,0:T(8,128)(2,1)} %get-tuple-element.175, bf16[8,1024,1024]{2,1,0:T(8,128)(2,1)} %get-tuple-element.174, s32[]{:T(128)} %get-tuple-element.160), kind=kOutput, calls=%fused_computation.133.clone.1 | convolution fusion | flops 2148531200 | bytes 8393216 | tf_op jit(solution)/shard_map/while/body/eval_jaxpr/dot_general | solution.py:58
  221.8 4.7 %fusion.87 = (f32[1024]{0:T(1024)S(1)}, f32[1024,1024]{0,1:T(8,128)S(1)}) fusion(bf16[1024,1024]{1,0:T(8,128)(2,1)} %get-tuple-element.175, bf16[8,1024,1024]{2,1,0:T(8,128)(2,1)} %get-tuple-element.174, s32[]{:T(128)} %get-tuple-element.160), kind=kOutput, calls=%fused_computation.133.clone.1 | convolution fusion | flops 2148531200 | bytes 8393216 | tf_op jit(solution)/shard_map/while/body/eval_jaxpr/dot_general | solution.py:58
  228.5 11.0 %all-gather.4 = f32[4,3,8192]{2,1,0:T(4,128)S(1)} all-gather(f32[1,3,8192]{2,1,0:T(4,128)S(1)} %maximum_bitcast_fusion), channel_id=2, replica_groups=mesh['dp'=4,'expert_0'=4,'expert_1'=4,'expert_2'=2] {'expert_0'}, dimensions={0}, use_global_device_ids=true | all-gather | bytes 491520 | tf_op jit(solution)/shard_map/all_gather | solution.py:28
  240.1 9.9 %all-gather.5 = f32[4,3,8192]{2,1,0:T(4,128)S(1)} all-gather(f32[1,3,8192]{2,1,0:T(4,128)S(1)} %maximum_bitcast_fusion.1), channel_id=3, replica_groups=mesh['dp'=4,'expert_0'=4,'expert_1'=4,'expert_2'=2] {'expert_1'}, dimensions={0}, use_global_device_ids=true | all-gather | bytes 491520 | tf_op jit(solution)/shard_map/all_gather | solution.py:28
  250.5 6.9 %all-gather.6 = f32[2,3,8192]{2,1,0:T(4,128)S(1)} all-gather(f32[1,3,8192]{2,1,0:T(4,128)S(1)} %maximum_bitcast_fusion.2), channel_id=4, replica_groups=mesh['dp'=4,'expert_0'=4,'expert_1'=4,'expert_2'=2] {'expert_2'}, dimensions={0}, use_global_device_ids=true | all-gather | bytes 294912 | tf_op jit(solution)/shard_map/all_gather | solution.py:28
  258.7 8.4 %all-reduce.2 = (f32[512]{0:T(512)S(1)}, f32[512]{0:T(512)S(1)}) all-reduce(f32[512]{0:T(512)S(1)} %convert_reduce_fusion, f32[512]{0:T(512)S(1)} %bitcast.294), channel_id=1, replica_groups=mesh['dp'=4,'expert_0'=4,'expert_1'=4,'expert_2'=2] {'dp'}, use_global_device_ids=true, to_apply=%region_16.17 | all-reduce | flops 1024 | bytes 8192 | tf_op jit(solution)/shard_map/psum | solution.py:48
  267.2 8.7 %all-reduce.1 = (f32[512]{0:T(512)S(1)}, f32[512]{0:T(512)S(1)}) all-reduce(f32[512]{0:T(512)S(1)} %get-tuple-element.71, f32[512]{0:T(512)S(1)} %get-tuple-element.72), channel_id=1, replica_groups=mesh['dp'=4,'expert_0'=4,'expert_1'=4,'expert_2'=2] {'expert_0'}, use_global_device_ids=true, to_apply=%region_17.18 | all-reduce | flops 1024 | bytes 8192 | tf_op jit(solution)/shard_map/psum | solution.py:48
  275.8 6.3 %all-reduce = (f32[512]{0:T(512)S(1)}, f32[512]{0:T(512)S(1)}) all-reduce(f32[512]{0:T(512)S(1)} %get-tuple-element.69, f32[512]{0:T(512)S(1)} %get-tuple-element.70), channel_id=1, replica_groups=mesh['dp'=4,'expert_0'=4,'expert_1'=4,'expert_2'=2] {'expert_1'}, use_global_device_ids=true, to_apply=%region_18.19 | all-reduce | flops 1024 | bytes 8192 | tf_op jit(solution)/shard_map/psum | solution.py:48
  282.1 8.5 %all-reduce.3 = (f32[512]{0:T(512)S(1)}, f32[512]{0:T(512)S(1)}) all-reduce(f32[512]{0:T(512)S(1)} %get-tuple-element.67, f32[512]{0:T(512)S(1)} %get-tuple-element.68), channel_id=1, replica_groups=mesh['dp'=4,'expert_0'=4,'expert_1'=4,'expert_2'=2] {'expert_2'}, use_global_device_ids=true, to_apply=%region_19.20 | all-reduce | flops 1024 | bytes 8192 | tf_op jit(solution)/shard_map/psum | solution.py:48
  (124 shorter events, 35.1 us)
Async XLA Ops:
  7.2 67.2 %copy-start = (bf16[1024,64]{0,1:T(8,128)(2,1)S(1)}, bf16[1024,64]{0,1:T(8,128)(2,1)}, u32[]{:S(2)}) copy-start(bf16[1024,64]{0,1:T(8,128)(2,1)} %param.15) | copy-start | bytes 393220
  11.3 40.7 %copy-start.7 = (bf16[2,1024,1024]{2,1,0:T(8,128)(2,1)S(1)}, bf16[2,1024,1024]{2,1,0:T(8,128)(2,1)}, u32[]{:S(2)}) copy-start(bf16[2,1024,1024]{2,1,0:T(8,128)(2,1)} %param.16) | copy-start | bytes 12582916
  67.0 7.3 %copy-start.1 = (bf16[256,1024]{1,0:T(8,128)(2,1)S(1)}, bf16[256,1024]{1,0:T(8,128)(2,1)}, u32[]{:S(2)}) copy-start(bf16[256,1024]{1,0:T(8,128)(2,1)} %param.13) | copy-start | bytes 1572868
  67.0 7.3 %copy-start.8 = (f32[1024]{0:T(1024)S(1)}, f32[1024]{0:T(1024)}, u32[]{:S(2)}) copy-start(f32[1024]{0:T(1024)} %param.14) | copy-start | bytes 12292
  67.0 7.7 %copy-start.2 = (s32[256,2]{0,1:T(2,128)S(1)}, s32[256,2]{0,1:T(2,128)}, u32[]{:S(2)}) copy-start(s32[256,2]{0,1:T(2,128)} %param.23) | copy-start | bytes 6148
  70.4 32.3 %all-to-all-start.1 = ((bf16[32,2,16,1024]{3,2,1,0:T(8,128)(2,1)}), bf16[32,2,16,1024]{3,2,1,0:T(8,128)(2,1)S(1)}, u32[]{:S(2)}, u32[]{:S(2)}) async-start(bf16[32,2,16,1024]{3,2,1,0:T(8,128)(2,1)} %copy.53), calls=%async_computation.1 | async-start | bytes 4194304 | tf_op jit(solution)/shard_map/all_to_all | solution.py:141
  74.3 101.9 %all-gather.9.cloned.1.call-start = ((), (), s32[]{:S(2)}) async-start(), calls=%async_computation.2 | async-start | bytes 17301504 | tf_op jit(solution)/shard_map/all_gather | solution.py:153
  102.6 1.7 copy-start.4
  103.4 2.0 copy-start.6
  103.4 5.3 %copy-start.3 = (s32[256]{0:T(256)S(1)}, s32[256]{0:T(256)}, u32[]{:S(2)}) copy-start(s32[256]{0:T(256)} %param.22) | copy-start | bytes 3076
  105.9 5.5 %collective-permute-start.1 = (s32[1]{0:T(128)}, s32[1]{0:T(128)}, u32[]{:S(2)}, u32[]{:S(2)}) collective-permute-start(s32[1]{0:T(128)} %slice.204), channel_id=1, source_target_pairs={{1,0},{2,1},{3,2},{4,3},{5,4},{6,5},{7,6},{8,7},{9,8},{10,9},{11,1... | collective-permute-start | bytes 20 | tf_op jit(solution)/shard_map/ppermute | solution.py:17
  109.2 148.4 %collective-permute-start = (s32[1]{0:T(128)}, s32[1]{0:T(128)}, u32[]{:S(2)}, u32[]{:S(2)}) collective-permute-start(s32[1]{0:T(128)} %slice.194), channel_id=1, source_target_pairs={{1,0},{2,1},{3,2},{4,3},{5,4},{6,5},{7,6},{8,7},{9,8},{10,9},{11,1... | collective-permute-start | bytes 20 | tf_op jit(solution)/shard_map/ppermute | solution.py:17
  258.4 34.1 %copy-start.5 = (f32[256]{0:T(256)}, f32[256]{0:T(256)S(1)}, u32[]{:S(2)}) copy-start(f32[256]{0:T(256)S(1)} %compare_select_fusion) | copy-start | bytes 3076
Sparse Core Ops, SparseCore 0:
  105.5 70.7 all-gather.8
where the time goes:
time: 300 us; the launch traced here: 299 us
  blocking collectives  121 us (40%)
  waiting for transfers between devices  67.7 us (23%)
  matrix products  56.8 us (19%)
  other arithmetic  20.3 us (7%)
  between operations  15 us (5%)
  local copies, waits for them, and re-layouts  9.12 us (3%)
  starting transfers between devices  8.66 us (3%)
    all_gather x1, waiting for transfers between devices, local(): lax.all_gather(final_rows, EXPERT, axis=0, tiled=True)  39.9 us
    dot_general x8, matrix products, stats_block(): jnp.dot(hidden_rows, vocab_weight, preferred_element_type=jnp.float32)  37.5 us
    all_to_all x1, blocking collectives, local(): lax.all_to_all(outgoing, EXPERT, split_axis=0, concat_axis=0, tiled=True)  37.4 us
    psum x4, blocking collectives, by_axis(): value = lax.psum(value, axis)  31.9 us
    all_to_all x1, waiting for transfers between devices, local(): lax.all_to_all(expert_result, EXPERT, split_axis=0, concat_axis=0, tiled=...  27.8 us
    all_gather x3, blocking collectives, gathered_once(): both, at, found = (lax.all_gather(jnp.concatenate(lines), axis), 0, {})  27.8 us
    all_gather x1, blocking collectives, local(): lax.all_gather(targets, EXPERT, axis=0, tiled=True)  24.1 us
    reduce_sum x8, other arithmetic, stats_block(): picked = jnp.sum(jnp.where(columns == wanted[:, None], scores, 0.0), axis=1)  11.3 us
  transfers between devices with their start and end apart: 4, of which 2 were waited for; matrix products, arithmetic and copies ran while one was open for 19% of the time, Pallas kernels for 0%

commit v1 on v0

--- a/solution.py
+++ b/solution.py
@@ -150,7 +150,9 @@
     counted = jnp.concatenate([doc_ids[1:], following[1]]) == doc_ids
     voc_start = lax.axis_index(EXPERT) * vocab_weight.shape[1]
     fresh = row_stats(
-        lax.all_gather(final_rows, EXPERT, axis=0, tiled=True),
+        jnp.concatenate(
+            lax.all_to_all(jnp.stack([final_rows] * lax.axis_size(EXPERT)), EXPERT, 0, 0), axis=0
+        ),
         lax.all_gather(targets, EXPERT, axis=0, tiled=True),
         vocab_weight,
         voc_start,

time: 300 us -> 507 us (1.69)
  waiting for transfers between devices: 67.7 us -> 211 us
  blocking collectives: 121 us -> 193 us
  between operations: 15 us -> 1.63 us
  local copies, waits for them, and re-layouts: 9.12 us -> 15.2 us
  starting transfers between devices: 8.66 us -> 13.9 us
    ppermute x2, waiting for transfers between devices: 0.01 us -> 183 us  [shifted(): lax.ppermute(value, axis, [(source, source + steps) for source in range(f...]
    all_gather x1, blocking collectives: 24.1 us -> 93.7 us  [local(): lax.all_gather(targets, EXPERT, axis=0, tiled=True)]
    all_gather x1 -> x0, waiting for transfers between devices: 39.9 us -> none  [local(): lax.all_gather(final_rows, EXPERT, axis=0, tiled=True)]
    another operation x1 -> x2, local copies, waits for them, and re-layouts: 0.01 us -> 6 us  [the longest x1 6 us: local(): jnp.stack([final_rows] * lax.axis_size(EXPERT))]
    all_to_all x0 -> x1, starting transfers between devices: none -> 5.73 us  [local(): lax.all_to_all(jnp.stack([final_rows] * lax.axis_size(EXPERT)), EXPERT, 0...]
  transfers between devices with their start and end apart: 4 -> 4, of which waited for: 2 -> 2; matrix products, arithmetic and copies ran while one was open for 19% -> 10% of each run, Pallas kernels for 0% -> 0%
where the time goes in v1:
time: 507 us; the launch traced here: 506 us
  waiting for transfers between devices  211 us (42%)
  blocking collectives  193 us (38%)
  matrix products  51.8 us (10%)
  other arithmetic  19.4 us (4%)
  local copies, waits for them, and re-layouts  15.2 us (3%)
  starting transfers between devices  13.9 us (3%)
    ppermute x2, waiting for transfers between devices, shifted(): lax.ppermute(value, axis, [(source, source + steps) for source in range(f...  183 us
    all_gather x1, blocking collectives, local(): lax.all_gather(targets, EXPERT, axis=0, tiled=True)  93.7 us
    all_to_all x1, blocking collectives, local(): lax.all_to_all(outgoing, EXPERT, split_axis=0, concat_axis=0, tiled=True)  37.4 us
    psum x4, blocking collectives, by_axis(): value = lax.psum(value, axis)  32.7 us
    dot_general x8, matrix products, stats_block(): jnp.dot(hidden_rows, vocab_weight, preferred_element_type=jnp.float32)  32.5 us
    all_gather x3, blocking collectives, gathered_once(): both, at, found = (lax.all_gather(jnp.concatenate(lines), axis), 0, {})  29.2 us
    all_to_all x1, waiting for transfers between devices, local(): lax.all_to_all(expert_result, EXPERT, split_axis=0, concat_axis=0, tiled=...  27.9 us
    reduce_sum x8, other arithmetic, stats_block(): picked = jnp.sum(jnp.where(columns == wanted[:, None], scores, 0.0), axis=1)  11.3 us
  transfers between devices with their start and end apart: 4, of which 2 were waited for; matrix products, arithmetic and copies ran while one was open for 10% of the time, Pallas kernels for 0%

profile of v1, /device:TPU:1, one launch (start us, length us, event | category | flops | bytes accessed | tf_op | source)
XLA Modules:
  0.0 506.2 jit_solution(17490194737310076174)
XLA Ops:
  8.1 37.4 %all_to_all.15 = bf16[32,2,16,1024]{3,2,1,0:T(8,128)(2,1)S(1)} all-to-all(bf16[32,2,16,1024]{3,2,1,0:T(8,128)(2,1)S(1)} %bitcast.274), channel_id=1, replica_groups=mesh['dp'=4,'expert_0'=4,'expert_1'=4,'expert_2'=2] {'expert_0','expert_..., dimensions={0} | all-to-all | bytes 4194304 | tf_op jit(solution)/shard_map/all_to_all | solution.py:132
  45.5 4.3 fusion.8
  49.8 10.7 %convert_bitcast_fusion = bf16[32,2,16,1024]{3,2,0,1:T(8,128)(2,1)} fusion(bf16[2,1024,1024]{2,1,0:T(8,128)(2,1)} %param.18, f32[2,32,16,1024]{3,2,1,0:T(8,128)} %fusion.8, bf16[2,1024,1024]{2,1,0:T(8,128)(2,1)} %param.17, bf16[32,2,16,1024]{3,2,1,0:T(8,128)(2,1)S(1)} %all_to_all.15), kind=kOutput, calls=%fused_computation.21 | convolution fusion | flops 4302307328 | bytes 16777216 | tf_op jit(solution)/shard_map/sekf,efd->sekd/dot_general | solution.py:138
  68.2 27.9 %all-to-all-done.1 = bf16[32,2,16,1024]{3,2,1,0:T(8,128)(2,1)S(1)} async-done(((bf16[32,2,16,1024]{3,2,1,0:T(8,128)(2,1)}), bf16[32,2,16,1024]{3,2,1,0:T(8,128)(2,1)S(1)}, u32[]{:S(2)}, u32[]{:S(2)}) %all-to-all-start.1) | async-done | bytes 2097184 | tf_op jit(solution)/shard_map/all_to_all | solution.py:141
  98.0 6.0 %stack.2 = bf16[32,256,1024]{2,1,0:T(8,128)(2,1)} broadcast(bf16[256,1024]{1,0:T(8,128)(2,1)S(1)} %multiply_convert_fusion), dimensions={1,2} | broadcast | bytes 17301504 | tf_op jit(solution)/shard_map/stack | solution.py:154
  104.0 5.7 %all-to-all-start.2 = ((bf16[32,256,1024]{2,1,0:T(8,128)(2,1)}), bf16[32,256,1024]{2,1,0:T(8,128)(2,1)}, u32[]{:S(2)}, u32[]{:S(2)}) async-start(bf16[32,256,1024]{2,1,0:T(8,128)(2,1)} %stack.2), calls=%async_computation.2 | async-start | bytes 33554432 | tf_op jit(solution)/shard_map/all_to_all | solution.py:154
  115.4 182.9 %collective-permute-done.1 = s32[1]{0:T(128)} collective-permute-done((s32[1]{0:T(128)}, s32[1]{0:T(128)}, u32[]{:S(2)}, u32[]{:S(2)}) %collective-permute-start.1) | collective-permute-done | bytes 36 | tf_op jit(solution)/shard_map/ppermute | solution.py:17
  299.0 93.7 %all-gather.3 = s32[32,1,256]{2,1,0:T(1,128)S(1)} all-gather(s32[1,1,256]{2,1,0:T(1,128)S(1)} %bitcast.293), channel_id=1, replica_groups=mesh['dp'=4,'expert_0'=4,'expert_1'=4,'expert_2'=2] {'expert_0','expert_..., dimensions={0}, use_global_device_ids=true | all-gather | bytes 33792 | tf_op jit(solution)/shard_map/all_gather | solution.py:156
  392.8 47.1 %while.14 = (s32[]{:T(128)}, f32[8,1024]{1,0:T(8,128)S(1)}, f32[8,1024]{1,0:T(8,128)S(1)}, f32[8,1024]{1,0:T(8,128)S(1)}, bf16[8,1024,1024]{2,1,0:T(8,128)(2,1)}...) while((s32[]{:T(128)}, f32[8,1024]{1,0:T(8,128)S(1)}, ...), condition=%wide.region_10.11_spmd, body=%wide.region_6.10_spmd.sunk | while | flops 2153773056 | bytes 12644985 | solution.py:72
  392.8 4.1 fusion.87
  398.7 4.1 fusion.87
  404.6 4.1 fusion.87
  410.5 4.1 fusion.87
  416.4 4.1 fusion.87
  422.3 4.1 fusion.87
  428.1 4.1 fusion.87
  434.0 4.1 fusion.87
  440.1 12.8 %all-gather.4 = f32[4,3,8192]{2,1,0:T(4,128)S(1)} all-gather(f32[1,3,8192]{2,1,0:T(4,128)S(1)} %maximum_bitcast_fusion), channel_id=2, replica_groups=mesh['dp'=4,'expert_0'=4,'expert_1'=4,'expert_2'=2] {'expert_0'}, dimensions={0}, use_global_device_ids=true | all-gather | bytes 491520 | tf_op jit(solution)/shard_map/all_gather | solution.py:28
  453.5 10.4 %all-gather.5 = f32[4,3,8192]{2,1,0:T(4,128)S(1)} all-gather(f32[1,3,8192]{2,1,0:T(4,128)S(1)} %maximum_bitcast_fusion.1), channel_id=3, replica_groups=mesh['dp'=4,'expert_0'=4,'expert_1'=4,'expert_2'=2] {'expert_1'}, dimensions={0}, use_global_device_ids=true | all-gather | bytes 491520 | tf_op jit(solution)/shard_map/all_gather | solution.py:28
  464.5 5.9 %all-gather.6 = f32[2,3,8192]{2,1,0:T(4,128)S(1)} all-gather(f32[1,3,8192]{2,1,0:T(4,128)S(1)} %maximum_bitcast_fusion.2), channel_id=4, replica_groups=mesh['dp'=4,'expert_0'=4,'expert_1'=4,'expert_2'=2] {'expert_2'}, dimensions={0}, use_global_device_ids=true | all-gather | bytes 294912 | tf_op jit(solution)/shard_map/all_gather | solution.py:28
  471.6 8.7 %all-reduce.2 = (f32[512]{0:T(512)S(1)}, f32[512]{0:T(512)S(1)}) all-reduce(f32[512]{0:T(512)S(1)} %convert_reduce_fusion, f32[512]{0:T(512)S(1)} %bitcast.294), channel_id=1, replica_groups=mesh['dp'=4,'expert_0'=4,'expert_1'=4,'expert_2'=2] {'dp'}, use_global_device_ids=true, to_apply=%region_16.17 | all-reduce | flops 1024 | bytes 8192 | tf_op jit(solution)/shard_map/psum | solution.py:48
  480.4 9.1 %all-reduce.1 = (f32[512]{0:T(512)S(1)}, f32[512]{0:T(512)S(1)}) all-reduce(f32[512]{0:T(512)S(1)} %get-tuple-element.71, f32[512]{0:T(512)S(1)} %get-tuple-element.72), channel_id=1, replica_groups=mesh['dp'=4,'expert_0'=4,'expert_1'=4,'expert_2'=2] {'expert_0'}, use_global_device_ids=true, to_apply=%region_17.18 | all-reduce | flops 1024 | bytes 8192 | tf_op jit(solution)/shard_map/psum | solution.py:48
  489.5 6.3 %all-reduce = (f32[512]{0:T(512)S(1)}, f32[512]{0:T(512)S(1)}) all-reduce(f32[512]{0:T(512)S(1)} %get-tuple-element.69, f32[512]{0:T(512)S(1)} %get-tuple-element.70), channel_id=1, replica_groups=mesh['dp'=4,'expert_0'=4,'expert_1'=4,'expert_2'=2] {'expert_1'}, use_global_device_ids=true, to_apply=%region_18.19 | all-reduce | flops 1024 | bytes 8192 | tf_op jit(solution)/shard_map/psum | solution.py:48
  495.8 8.5 %all-reduce.3 = (f32[512]{0:T(512)S(1)}, f32[512]{0:T(512)S(1)}) all-reduce(f32[512]{0:T(512)S(1)} %get-tuple-element.67, f32[512]{0:T(512)S(1)} %get-tuple-element.68), channel_id=1, replica_groups=mesh['dp'=4,'expert_0'=4,'expert_1'=4,'expert_2'=2] {'expert_2'}, use_global_device_ids=true, to_apply=%region_19.20 | all-reduce | flops 1024 | bytes 8192 | tf_op jit(solution)/shard_map/psum | solution.py:48
  (128 shorter events, 41.1 us)
Async XLA Ops:
  0.6 67.1 %copy-start = (bf16[1024,64]{0,1:T(8,128)(2,1)S(1)}, bf16[1024,64]{0,1:T(8,128)(2,1)}, u32[]{:S(2)}) copy-start(bf16[1024,64]{0,1:T(8,128)(2,1)} %param.15) | copy-start | bytes 393220
  4.8 40.7 %copy-start.8 = (bf16[2,1024,1024]{2,1,0:T(8,128)(2,1)S(1)}, bf16[2,1024,1024]{2,1,0:T(8,128)(2,1)}, u32[]{:S(2)}) copy-start(bf16[2,1024,1024]{2,1,0:T(8,128)(2,1)} %param.16) | copy-start | bytes 12582916
  60.5 7.3 %copy-start.2 = (bf16[256,1024]{1,0:T(8,128)(2,1)S(1)}, bf16[256,1024]{1,0:T(8,128)(2,1)}, u32[]{:S(2)}) copy-start(bf16[256,1024]{1,0:T(8,128)(2,1)} %param.13) | copy-start | bytes 1572868
  60.5 7.3 %copy-start.10 = (f32[1024]{0:T(1024)S(1)}, f32[1024]{0:T(1024)}, u32[]{:S(2)}) copy-start(f32[1024]{0:T(1024)} %param.14) | copy-start | bytes 12292
  60.5 7.7 %copy-start.3 = (s32[256,2]{0,1:T(2,128)S(1)}, s32[256,2]{0,1:T(2,128)}, u32[]{:S(2)}) copy-start(s32[256,2]{0,1:T(2,128)} %param.23) | copy-start | bytes 6148
  63.8 32.3 %all-to-all-start.1 = ((bf16[32,2,16,1024]{3,2,1,0:T(8,128)(2,1)}), bf16[32,2,16,1024]{3,2,1,0:T(8,128)(2,1)S(1)}, u32[]{:S(2)}, u32[]{:S(2)}) async-start(bf16[32,2,16,1024]{3,2,1,0:T(8,128)(2,1)} %copy.53), calls=%async_computation.1 | async-start | bytes 4194304 | tf_op jit(solution)/shard_map/all_to_all | solution.py:141
  96.1 1.7 copy-start.5
  104.0 5.7 %copy-start.7 = (s32[256]{0:T(256)S(1)}, s32[256]{0:T(256)}, u32[]{:S(2)}) copy-start(s32[256]{0:T(256)} %param.21) | copy-start | bytes 3076
  104.0 8.7 %copy-start.4 = (s32[256]{0:T(256)S(1)}, s32[256]{0:T(256)}, u32[]{:S(2)}) copy-start(s32[256]{0:T(256)} %param.22) | copy-start | bytes 3076
  104.0 288.8 %copy-start.9 = (bf16[1024,1024]{1,0:T(8,128)(2,1)S(1)}, bf16[1024,1024]{1,0:T(8,128)(2,1)}, u32[]{:S(2)}) copy-start(bf16[1024,1024]{1,0:T(8,128)(2,1)} %param.20) | copy-start | bytes 6291460
  104.0 288.8 %all-to-all-start.2 = ((bf16[32,256,1024]{2,1,0:T(8,128)(2,1)}), bf16[32,256,1024]{2,1,0:T(8,128)(2,1)}, u32[]{:S(2)}, u32[]{:S(2)}) async-start(bf16[32,256,1024]{2,1,0:T(8,128)(2,1)} %stack.2), calls=%async_computation.2 | async-start | bytes 33554432 | tf_op jit(solution)/shard_map/all_to_all | solution.py:154
  110.3 188.0 %collective-permute-start.1 = (s32[1]{0:T(128)}, s32[1]{0:T(128)}, u32[]{:S(2)}, u32[]{:S(2)}) collective-permute-start(s32[1]{0:T(128)} %slice.204), channel_id=1, source_target_pairs={{1,0},{2,1},{3,2},{4,3},{5,4},{6,5},{7,6},{8,7},{9,8},{10,9},{11,1... | collective-permute-start | bytes 20 | tf_op jit(solution)/shard_map/ppermute | solution.py:17
  113.2 357.4 %collective-permute-start = (s32[1]{0:T(128)}, s32[1]{0:T(128)}, u32[]{:S(2)}, u32[]{:S(2)}) collective-permute-start(s32[1]{0:T(128)} %slice.194), channel_id=1, source_target_pairs={{1,0},{2,1},{3,2},{4,3},{5,4},{6,5},{7,6},{8,7},{9,8},{10,9},{11,1... | collective-permute-start | bytes 20 | tf_op jit(solution)/shard_map/ppermute | solution.py:17
  439.9 66.3 %copy-start.1 = (bf16[1024,64]{0,1:T(8,128)(2,1)S(1)}, bf16[1024,64]{0,1:T(8,128)(2,1)}, u32[]{:S(2)}) copy-start(bf16[1024,64]{0,1:T(8,128)(2,1)} %param.15) | copy-start | bytes 393220
  471.3 34.9 %copy-start.6 = (f32[256]{0:T(256)}, f32[256]{0:T(256)S(1)}, u32[]{:S(2)}) copy-start(f32[256]{0:T(256)S(1)} %compare_select_fusion) | copy-start | bytes 3076
